TPU v7x, 32 devices: a whole 2x2x4 slice. The times are simulated.
32 devices in a mesh: groups: 2 (over y), row: 8 (over z, x), col: 2 (over core).
Axes of the slice: x: 2, y: 2, z: 4, core: 2. Of those that a mesh axis runs over, the one named last changes fastest.
Arguments:
- sigma_anc: bfloat16 [16384, 8192], P(('groups', 'row'), 'col'), parts along dimension 0, as said below
- panel: bfloat16 [16384, 3072], P(('groups', 'row'), 'col'), parts along dimension 0
- holder: int32 [128], P('groups'), parts along dimension 0, may hold values from 0 to 63, each once
- dinv_diag: float32 [6144], P(('groups', 'col')), parts along dimension 0, may hold values from 0.5 to 2
Outputs:
- sigma_aj: bfloat16 [16384, 3072], P(('groups', 'row'), 'col'), parts along dimension 0
- variances: float32 [6144], P(('groups', 'col')), parts along dimension 0
There are 2 independent parts, one for each index of `groups`. A program takes and returns all parts, laid end to end along the dimension named above; each array names one. Nothing has to cross between parts.
Inputs may be any that keep to these rules, and one draw needn't show every extreme that they name: holder is a permutation of the 64 tiles. sigma_anc is symmetric and positive definite.
All inputs are finite; a program needn't handle non-finite values.
Results may differ from a plain program's by a relative error of at most 0.001.
Values may be sent and summed in bfloat16 or wider, within the bound.
A program may use at most 128 MiB of HBM per device.

v0:
```python
import jax
import jax.numpy as jnp
from jax import lax
from jax.sharding import PartitionSpec as P

TILE = 128


def body(sigma_anc, panel, holder, dinv_diag):
    whole_rows = lax.all_gather(sigma_anc, "col", axis=1, tiled=True)
    local_rows = whole_rows.shape[0]
    width = whole_rows.shape[1]
    n_tiles = width // TILE
    per_dev = local_rows // TILE
    cols = panel.shape[1]
    position = lax.axis_index("row")
    my_tiles = lax.dynamic_slice_in_dim(holder, position * per_dev, per_dev)
    piece = lax.all_gather(panel, "row", axis=0, tiled=True)
    count = piece.shape[0]
    count_tiles = count // TILE
    ids = jnp.arange(count_tiles, dtype=jnp.int32)
    select = (holder[:, None] == ids[None, :]).astype(jnp.bfloat16)
    blocks = whole_rows.reshape(local_rows, n_tiles, TILE)
    picked = jnp.einsum("rtk,ts->rsk", blocks, select, preferred_element_type=jnp.float32)
    total = jnp.dot(
        picked.astype(jnp.bfloat16).reshape(local_rows, count),
        piece,
        preferred_element_type=jnp.float32,
    )
    count_tiles = count // TILE
    ids = jnp.arange(count_tiles, dtype=jnp.int32)
    select = (my_tiles[:, None] == ids[None, :]).astype(jnp.bfloat16)
    mine = jnp.einsum(
        "ji,irc->jrc",
        select,
        piece.reshape(count_tiles, TILE, cols),
        preferred_element_type=jnp.float32,
    )
    prod, mine = (total, mine)
    sigma_aj = (-prod).astype(jnp.bfloat16)
    partial_sums = jnp.sum(mine.reshape(local_rows, cols) * prod, axis=0)
    variances = dinv_diag + lax.psum(partial_sums, "row")
    return (sigma_aj, variances)


def solution(mesh):
    placed = (
        P(("groups", "row"), "col"),
        P(("groups", "row"), "col"),
        P("groups"),
        P(("groups", "col")),
    )
    return jax.shard_map(
        body,
        mesh=mesh,
        in_specs=placed,
        out_specs=(P(("groups", "row"), "col"), P(("groups", "col"))),
        check_vma=False,
    )
```

profile of v0, /device:TPU:0, one launch (start us, length us, event | category | flops | bytes accessed | tf_op | source)
XLA Modules:
  0.0 658.9 jit_solution(1104403360409697012)
XLA Ops:
  7.2 0.0 all-gather.3.cloned.1.call-start
  7.2 0.7 all-gather.3.cloned.1.call-update
  7.9 0.0 all-gather.5.cloned.1.call-start
  7.9 0.7 all-gather.5.cloned.1.call-update
  8.7 0.7 dynamic_slice.3
  9.4 33.0 %all-gather.3.cloned.1.call-done = bf16[1024,8192]{1,0:T(8,128)(2,1)} async-done(((bf16[1024,4096]{1,0:T(8,128)(2,1)}), bf16[1024,8192]{1,0:T(8,128)(2,1)}) %all-gather.3.cloned.1.call-update) | async-done | bytes 16777232 | tf_op jit(solution)/shard_map/all_gather | solution.py:10
  42.4 0.0 copy-start.1
  42.4 15.3 %copy.9 = bf16[128,8,64,128]{3,2,1,0:T(8,128)(2,1)} copy(bf16[128,8,64,128]{3,1,2,0:T(8,128)(2,1)} %bitcast.25) | data formatting | bytes 33554432
  57.6 0.0 copy-done.1
  57.6 11.5 %convolution_convert_fusion = bf16[64,1024,128]{2,0,1:T(8,128)(2,1)} fusion(bf16[1024,64,128]{2,1,0:T(8,128)(2,1)} %bitcast.22, s32[64]{0:T(128)S(1)} %copy-done.1), kind=kOutput, calls=%fused_computation.5 | convolution fusion | flops 1082134528 | bytes 33554688 | tf_op jit(solution)/shard_map/rtk,ts->rsk/dot_general | solution.py:24
  69.1 456.3 %all-gather.5.cloned.1.call-done = bf16[8192,1536]{1,0:T(8,128)(2,1)} async-done(((bf16[1024,1536]{1,0:T(8,128)(2,1)}), bf16[8192,1536]{1,0:T(8,128)(2,1)}) %all-gather.5.cloned.1.call-update) | async-done | bytes 25165840 | tf_op jit(solution)/shard_map/all_gather | solution.py:18
  525.5 38.6 %fusion = f32[8,128,1536]{2,0,1:T(8,128)S(1)} fusion(bf16[64,128,1536]{2,1,0:T(8,128)(2,1)} %bitcast.24, s32[8]{0:T(128)S(1)} %dynamic_slice.3), kind=kOutput, calls=%fused_computation | convolution fusion | flops 201327104 | bytes 31457312 | tf_op jit(solution)/shard_map/ji,irc->jrc/dot_general | solution.py:33
  564.1 3.6 copy.8
  567.7 0.0 copy-start
  567.7 63.2 %fusion.5 = (f32[1536]{0:T(1024)S(1)}, bf16[1024,1536]{1,0:T(8,128)(2,1)}) fusion(f32[8,128,1536]{2,1,0:T(8,128)S(1)} %copy.8, bf16[8192,1536]{1,0:T(8,128)(2,1)} %all-gather.5.cloned.1.call-done, bf16[128,8,64,128]{3,2,1,0:T(8,128)(2,1)} %bitcast.23), kind=kOutput, calls=%fused_computation.7 | convolution fusion | flops 25776093184 | bytes 51386368 | tf_op jit(solution)/shard_map/dot_general | solution.py:25
  631.0 20.4 %psum.7 = f32[1536]{0:T(1024)S(1)} all-reduce(f32[1536]{0:T(1024)S(1)} %get-tuple-element.2), channel_id=1, replica_groups=mesh['groups'=2,'row'=8,'col'=2] {'row'}, use_global_device_ids=true, to_apply=%region_1.0 | all-reduce | flops 1536 | bytes 12288 | tf_op jit(solution)/shard_map/psum | solution.py:42
  651.4 0.0 copy-done
  651.4 0.6 add.9
Async XLA Ops:
  7.2 35.2 %all-gather.3.cloned.1.call-start = ((), (), s32[]{:S(2)}) async-start(), calls=%async_computation | async-start | bytes 25165824 | tf_op jit(solution)/shard_map/all_gather | solution.py:10
  7.9 517.6 %all-gather.5.cloned.1.call-start = ((), (), s32[]{:S(2)}) async-start(), calls=%async_computation.1 | async-start | bytes 28311552 | tf_op jit(solution)/shard_map/all_gather | solution.py:18
  42.4 15.3 %copy-start.1 = (s32[64]{0:T(128)S(1)}, s32[64]{0:T(128)}, u32[]{:S(2)}) copy-start(s32[64]{0:T(128)} %param.6) | copy-start | bytes 772
  567.7 83.7 %copy-start = (f32[1536]{0:T(1024)S(1)}, f32[1536]{0:T(1024)}, u32[]{:S(2)}) copy-start(f32[1536]{0:T(1024)} %param.7) | copy-start | bytes 18436
Sparse Core Ops, SparseCore 0:
  9.5 32.7 all-gather.2
  43.9 481.5 all-gather.4
where the time goes:
time: 659 us
  waiting for transfers between devices  491 us (75%)
  matrix products  113 us (17%)
  blocking collectives  20.4 us (3%)
  local copies, waits for them, and re-layouts  19.6 us (3%)
  between operations  14.1 us (2%)
    all_gather x1, waiting for transfers between devices, body(): piece = lax.all_gather(panel, 'row', axis=0, tiled=True)  456 us
    dot_general x1, matrix products, body(): jnp.dot(picked.astype(jnp.bfloat16).reshape(local_rows, count), piece, pr...  63.2 us
    dot_general x1, matrix products, body(): jnp.einsum('ji,irc->jrc', select, piece.reshape(count_tiles, TILE, cols),...  38.6 us
    all_gather x1, waiting for transfers between devices, body(): whole_rows = lax.all_gather(sigma_anc, 'col', axis=1, tiled=True)  33 us
    psum x1, blocking collectives, body(): variances = dinv_diag + lax.psum(partial_sums, 'row')  20.4 us
    unnamed x5, local copies, waits for them, and re-layouts  15.3 us
  transfers between devices with their start and end apart: 2, of which 2 were waited for; matrix products, arithmetic and copies ran while one was open for 4% of the time, Pallas kernels for 0%

commit v1 on v0

v1 whole, which is shorter than its diff:
```python
import functools

import jax
import jax.numpy as jnp
from jax import lax
from jax.experimental import pallas as pl
from jax.experimental.pallas import tpu as pltpu
from jax.sharding import PartitionSpec as P

MESH = pl.DeviceIdType.MESH


def block_of(size, most):
    block = min(size, most)
    while size % block:
        block -= 128
    return block


def kernel(n, nc, holder, logical, sigma, panel, out, sums, s, p, acc, staged, parts,
           own_sem, far_sem, near_sem, f_send, f_recv, b_send, b_recv, o_sem, v_send, v_recv):
    g = lax.axis_index("groups")
    r = lax.axis_index("row")
    c = lax.axis_index("col")
    per, tile, cols = panel.shape
    rows, width = sigma.shape
    tiles = p.shape[0]
    half = n // 2
    fwd = (per + 1) // 2
    bwd = per - fwd

    def row_of(at):
        at = lax.rem(at + 2 * n, n)
        odd = at // half
        return 2 * (at + odd * (2 * half - 1 - 2 * at)) + odd

    odd = lax.rem(r, 2)
    up = r // 2
    at = up + odd * (2 * half - 1 - 2 * up)
    after = (g, row_of(at + 1), c)
    before = (g, row_of(at - 1), c)

    barrier = pltpu.get_barrier_semaphore()

    def greet(k, carry):
        pl.semaphore_signal(barrier, 1, device_id=(g, lax.rem(r + k, n), c), device_id_type=MESH)
        return carry

    lax.fori_loop(1, n, greet, 0)
    for k in range(1, nc):
        pl.semaphore_signal(barrier, 1, device_id=(g, r, lax.rem(c + k, nc)), device_id_type=MESH)
    pl.semaphore_wait(barrier, n - 1 + nc - 1)

    def f_tile(k, i):
        return row_of(at - k) * per + i

    def b_tile(k, i):
        return row_of(at + k) * per + fwd + i

    def f_copy(k, i, src=None):
        t = f_tile(k, i)
        return pltpu.make_async_remote_copy(
            src_ref=p.at[t] if src is None else src, dst_ref=p.at[t],
            send_sem=f_send.at[k * fwd + i], recv_sem=f_recv.at[k * fwd + i],
            device_id=after, device_id_type=MESH)

    def b_copy(k, i, src=None):
        t = b_tile(k, i)
        return pltpu.make_async_remote_copy(
            src_ref=p.at[t] if src is None else src, dst_ref=p.at[t],
            send_sem=b_send.at[k * bwd + i], recv_sem=b_recv.at[k * bwd + i],
            device_id=before, device_id_type=MESH)

    def f_landed(k, i):
        t = f_tile(k, i)
        return pltpu.make_async_remote_copy(
            src_ref=p.at[t], dst_ref=p.at[t],
            send_sem=f_send.at[(k - 1) * fwd + i], recv_sem=f_recv.at[(k - 1) * fwd + i],
            device_id=after, device_id_type=MESH)

    def b_landed(k, i):
        t = b_tile(k, i)
        return pltpu.make_async_remote_copy(
            src_ref=p.at[t], dst_ref=p.at[t],
            send_sem=b_send.at[(k - 1) * bwd + i], recv_sem=b_recv.at[(k - 1) * bwd + i],
            device_id=before, device_id_type=MESH)

    for i in range(fwd):
        f_copy(0, i, panel.at[i]).start()
        if i < bwd:
            b_copy(0, i, panel.at[fwd + i]).start()

    held = width // tile

    def near(j):
        return pltpu.make_async_copy(
            sigma.at[:, pl.ds(pl.multiple_of(j * tile, tile), tile)], s.at[c * held + j], near_sem.at[j])

    def far(k, j):
        return pltpu.make_async_remote_copy(
            src_ref=sigma.at[:, pl.ds(pl.multiple_of(j * tile, tile), tile)], dst_ref=s.at[c * held + j],
            send_sem=far_sem.at[2 * k - 2, j], recv_sem=far_sem.at[2 * k - 1, j],
            device_id=(g, r, lax.rem(c + k, nc)), device_id_type=MESH)

    def far_landed(k, j):
        t = lax.rem(c + nc - k, nc) * held + j
        return pltpu.make_async_remote_copy(
            src_ref=s.at[t], dst_ref=s.at[t],
            send_sem=far_sem.at[2 * k - 2, j], recv_sem=far_sem.at[2 * k - 1, j],
            device_id=(g, r, lax.rem(c + k, nc)), device_id_type=MESH)

    def each(low, high, act):
        def step(k, carry):
            act(k)
            return carry
        lax.fori_loop(low, high, step, 0)

    for k in range(1, nc):
        each(0, held, lambda j: far(k, j).start())
    each(0, held, lambda j: near(j).start())
    own = pltpu.make_async_copy(panel, p.at[pl.ds(r * per, per)], own_sem)
    own.start()
    acc[...] = jnp.zeros_like(acc)
    own.wait()
    each(0, held, lambda j: near(j).wait())
    for k in range(1, nc):
        each(0, held, lambda j: far_landed(k, j).wait_recv())

    rb = block_of(rows, 512)
    cb = block_of(cols, 512)
    across = cols // cb

    def multiply(slots):
        columns = [logical[t] for t in slots]

        def block(q, carry):
            rs = pl.ds(pl.multiple_of((q // across) * rb, rb), rb)
            cs = pl.ds(pl.multiple_of(lax.rem(q, across) * cb, cb), cb)
            lhs = jnp.concatenate([s[w, rs, :] for w in columns], axis=1)
            rhs = jnp.concatenate([p[t, :, cs] for t in slots], axis=0)
            acc[rs, cs] += jnp.dot(lhs, rhs, preferred_element_type=jnp.float32)
            return carry

        lax.fori_loop(0, (rows // rb) * across, block, 0)

    def unit(u, carry):
        k = u // fwd
        i = lax.rem(u, fwd)

        @pl.when(k > 0)
        def _():
            f_landed(k, i).wait_recv()

            @pl.when(k < n - 1)
            def _():
                f_copy(k, i).start()

        if bwd == fwd:
            @pl.when(k > 0)
            def _():
                b_landed(k, i).wait_recv()

                @pl.when(k < n - 1)
                def _():
                    b_copy(k, i).start()

            multiply([f_tile(k, i), b_tile(k, i)])
        else:
            multiply([f_tile(k, i)])
            if bwd:
                @pl.when(i < bwd)
                def _():
                    @pl.when(k > 0)
                    def _():
                        b_landed(k, i).wait_recv()

                        @pl.when(k < n - 1)
                        def _():
                            b_copy(k, i).start()

                    multiply([b_tile(k, i)])
        return carry

    lax.fori_loop(0, n * fwd, unit, 0)

    def put(j):
        where = pl.ds(pl.multiple_of(j * tile, tile), tile)
        return pltpu.make_async_copy(staged.at[where], out.at[where], o_sem.at[j])

    parts[r] = jnp.zeros((1, cols), jnp.float32)

    def finish(j, carry):
        where = pl.ds(pl.multiple_of(j * tile, tile), tile)
        mine = p[holder[r * per + j]]
        for b in range(across):
            cs = pl.ds(b * cb, cb)
            prod = acc[where, cs]
            staged[where, cs] = (-prod).astype(staged.dtype)
            term = mine[:, b * cb:(b + 1) * cb].astype(jnp.float32) * prod
            parts[r, :, cs] += jnp.sum(term, axis=0, keepdims=True)
        put(j).start()
        return carry

    lax.fori_loop(0, per, finish, 0)

    def share(k):
        to = lax.rem(r + k, n)
        return pltpu.make_async_remote_copy(
            src_ref=parts.at[r], dst_ref=parts.at[r],
            send_sem=v_send.at[k - 1], recv_sem=v_recv.at[k - 1],
            device_id=(g, to, c), device_id_type=MESH)

    def gone(k):
        frm = lax.rem(r + n - k, n)
        return pltpu.make_async_remote_copy(
            src_ref=parts.at[frm], dst_ref=parts.at[frm],
            send_sem=v_send.at[k - 1], recv_sem=v_recv.at[k - 1],
            device_id=(g, lax.rem(r + k, n), c), device_id_type=MESH)

    each(1, n, lambda k: share(k).start())
    for k in range(1, nc):
        each(0, held, lambda j: far(k, j).wait_send())
    each(0, (n - 1) * fwd, lambda u: f_copy(u // fwd, lax.rem(u, fwd)).wait_send())
    if bwd:
        each(0, (n - 1) * bwd, lambda u: b_copy(u // bwd, lax.rem(u, bwd)).wait_send())
    each(0, per, lambda j: put(j).wait())
    each(1, n, lambda k: gone(k).wait_recv())
    each(1, n, lambda k: share(k).wait_send())
    total = parts[0]
    for k in range(1, n):
        total += parts[k]
    sums[...] = total


def body(n, nc, sigma_anc, panel, holder, dinv_diag):
    tiles = holder.shape[0]
    rows, width = sigma_anc.shape
    cols = panel.shape[1]
    per = tiles // n
    tile = panel.shape[0] // per
    fwd = (per + 1) // 2
    bwd = max(per - fwd, 1)
    ids = jnp.arange(tiles, dtype=jnp.int32)
    logical = jnp.sum(jnp.where(holder[:, None] == ids[None, :], ids[:, None], 0), axis=0, dtype=jnp.int32)
    dma = pltpu.SemaphoreType.DMA
    out, sums = pl.pallas_call(
        functools.partial(kernel, n, nc),
        out_shape=(
            jax.ShapeDtypeStruct((rows, cols), jnp.bfloat16),
            jax.ShapeDtypeStruct((1, cols), jnp.float32),
        ),
        in_specs=[
            pl.BlockSpec(memory_space=pltpu.SMEM),
            pl.BlockSpec(memory_space=pltpu.SMEM),
            pl.BlockSpec(memory_space=pl.ANY),
            pl.BlockSpec(memory_space=pl.ANY),
        ],
        out_specs=(
            pl.BlockSpec(memory_space=pl.ANY),
            pl.BlockSpec(memory_space=pltpu.VMEM),
        ),
        scratch_shapes=[
            pltpu.VMEM((width * nc // tile, rows, tile), sigma_anc.dtype),
            pltpu.VMEM((tiles, tile, cols), panel.dtype),
            pltpu.VMEM((rows, cols), jnp.float32),
            pltpu.VMEM((rows, cols), jnp.bfloat16),
            pltpu.VMEM((n, 1, cols), jnp.float32),
            dma,
            dma((2 * nc, width // tile)),
            dma((width // tile,)),
            dma((n * fwd,)),
            dma((n * fwd,)),
            dma((n * bwd,)),
            dma((n * bwd,)),
            dma((per,)),
            dma((n,)),
            dma((n,)),
        ],
        compiler_params=pltpu.CompilerParams(
            collective_id=0, has_side_effects=True, vmem_limit_bytes=60 << 20
        ),
    )(holder, logical, sigma_anc, panel.reshape(per, tile, cols))
    return out, dinv_diag + sums.reshape(cols)


def solution(mesh):
    placed = (
        P(("groups", "row"), "col"),
        P(("groups", "row"), "col"),
        P("groups"),
        P(("groups", "col")),
    )
    return jax.shard_map(
        functools.partial(body, mesh.shape["row"], mesh.shape["col"]),
        mesh=mesh,
        in_specs=placed,
        out_specs=(P(("groups", "row"), "col"), P(("groups", "col"))),
        check_vma=False,
    )
```

time: 659 us -> 261 us (0.40)
  waiting for transfers between devices: 491 us -> 0 us
  Pallas kernels: 0 us -> 254 us
  matrix products: 113 us -> 0 us
  blocking collectives: 20.4 us -> 0 us
  local copies, waits for them, and re-layouts: 19.6 us -> 3.76 us
  between operations: 14.1 us -> 0.65 us
    all_gather x2 -> x0, waiting for transfers between devices: 489 us -> none  [the longest x1 456 us: body(): piece = lax.all_gather(panel, 'row', axis=0, tiled=True)]
    pallas_call x0 -> x1, Pallas kernels: none -> 254 us  [body(): pl.pallas_call(functools.partial(kernel, n, nc), out_shape=(jax.ShapeDtyp...]
    dot_general x3 -> x0, matrix products: 113 us -> none  [the longest x1 63.2 us: body(): jnp.dot(picked.astype(jnp.bfloat16).reshape(local_rows, count), piece, pr...]
    psum x1 -> x0, blocking collectives: 20.4 us -> none  [body(): variances = dinv_diag + lax.psum(partial_sums, 'row')]
    unnamed x5 -> x3, local copies, waits for them, and re-layouts: 15.3 us -> 3.76 us
  transfers between devices with their start and end apart: 2 -> 0, of which waited for: 2 -> 0; matrix products, arithmetic and copies ran while one was open for 4% -> 0% of each run, Pallas kernels for 0% -> 0%
where the time goes in v1:
time: 261 us
  Pallas kernels  254 us (97%)
  local copies, waits for them, and re-layouts  3.76 us (1%)
    pallas_call x1, Pallas kernels, body(): pl.pallas_call(functools.partial(kernel, n, nc), out_shape=(jax.ShapeDtyp...  254 us

profile of v1, /device:TPU:0, one launch (start us, length us, event | category | flops | bytes accessed | tf_op | source)
XLA Modules:
  0.0 260.7 jit_solution(500267021186556892)
XLA Ops:
  0.6 1.3 select_reduce_fusion.logical
  1.9 0.0 copy-start
  1.9 253.7 %shard_map.59 = (bf16[1024,1536]{1,0:T(8,128)(2,1)}, f32[1,1536]{1,0:T(1,128)}) custom-call(s32[64]{0:T(128)} %holder.1, s32[64]{0:T(128)} %select_reduce_fusion.logical, bf16[1024,4096]{1,0:T(8,128)(2,1)} %sigma.1, bf16[8,128,1536]{2,1,0:T(8,128)(2,1)} %bitcast.1), custom_call_target="tpu_custom_call" | custom-call | tf_op jit(solution)/shard_map/pallas_call | solution.py:246
  255.6 0.7 reduce
  256.3 0.0 copy-done
  256.3 0.6 add.3
  256.9 3.8 %copy.7 = bf16[1024,1536]{1,0:T(8,128)(2,1)} copy(bf16[1024,1536]{1,0:T(8,128)(2,1)} %get-tuple-element.8) | data formatting | bytes 6291456
Async XLA Ops:
  1.9 254.4 %copy-start = (f32[1536]{0:T(1024)S(1)}, f32[1536]{0:T(1024)}, u32[]{:S(2)}) copy-start(f32[1536]{0:T(1024)} %param.7) | copy-start | bytes 18436

commit v2 on v1

--- a/solution.py
+++ b/solution.py
@@ -183,25 +183,18 @@
 
     lax.fori_loop(0, n * fwd, unit, 0)
 
-    def put(j):
-        where = pl.ds(pl.multiple_of(j * tile, tile), tile)
-        return pltpu.make_async_copy(staged.at[where], out.at[where], o_sem.at[j])
-
     parts[r] = jnp.zeros((1, cols), jnp.float32)
 
-    def finish(j, carry):
+    def weigh(j, carry):
         where = pl.ds(pl.multiple_of(j * tile, tile), tile)
         mine = p[holder[r * per + j]]
         for b in range(across):
             cs = pl.ds(b * cb, cb)
-            prod = acc[where, cs]
-            staged[where, cs] = (-prod).astype(staged.dtype)
-            term = mine[:, b * cb:(b + 1) * cb].astype(jnp.float32) * prod
+            term = mine[:, b * cb:(b + 1) * cb].astype(jnp.float32) * acc[where, cs]
             parts[r, :, cs] += jnp.sum(term, axis=0, keepdims=True)
-        put(j).start()
         return carry
 
-    lax.fori_loop(0, per, finish, 0)
+    lax.fori_loop(0, per, weigh, 0)
 
     def share(k):
         to = lax.rem(r + k, n)
@@ -218,6 +211,19 @@
             device_id=(g, lax.rem(r + k, n), c), device_id_type=MESH)
 
     each(1, n, lambda k: share(k).start())
+
+    def put(j):
+        where = pl.ds(pl.multiple_of(j * tile, tile), tile)
+        return pltpu.make_async_copy(staged.at[where], out.at[where], o_sem.at[j])
+
+    def finish(j, carry):
+        where = pl.ds(pl.multiple_of(j * tile, tile), tile)
+        staged[where, :] = (-acc[where, :]).astype(staged.dtype)
+        put(j).start()
+        return carry
+
+    lax.fori_loop(0, per, finish, 0)
+
     for k in range(1, nc):
         each(0, held, lambda j: far(k, j).wait_send())
     each(0, (n - 1) * fwd, lambda u: f_copy(u // fwd, lax.rem(u, fwd)).wait_send())

time: 261 us -> 261 us (level)
  no operation moved by 1% of the time
where the time goes in v2:
time: 261 us; the launch traced here: 260 us
  Pallas kernels  253 us (97%)
  local copies, waits for them, and re-layouts  3.76 us (1%)
    pallas_call x1, Pallas kernels, body(): pl.pallas_call(functools.partial(kernel, n, nc), out_shape=(jax.ShapeDtyp...  253 us

profile of v2, /device:TPU:0, one launch (start us, length us, event | category | flops | bytes accessed | tf_op | source)
XLA Modules:
  0.0 260.5 jit_solution(843686129106529932)
XLA Ops:
  0.6 1.3 select_reduce_fusion.logical
  1.9 0.0 copy-start
  1.9 253.5 %shard_map.59 = (bf16[1024,1536]{1,0:T(8,128)(2,1)}, f32[1,1536]{1,0:T(1,128)}) custom-call(s32[64]{0:T(128)} %holder.1, s32[64]{0:T(128)} %select_reduce_fusion.logical, bf16[1024,4096]{1,0:T(8,128)(2,1)} %sigma.1, bf16[8,128,1536]{2,1,0:T(8,128)(2,1)} %bitcast.1), custom_call_target="tpu_custom_call" | custom-call | tf_op jit(solution)/shard_map/pallas_call | solution.py:252
  255.4 0.7 reduce
  256.1 0.0 copy-done
  256.1 0.6 add.3
  256.7 3.8 %copy.7 = bf16[1024,1536]{1,0:T(8,128)(2,1)} copy(bf16[1024,1536]{1,0:T(8,128)(2,1)} %get-tuple-element.8) | data formatting | bytes 6291456
Async XLA Ops:
  1.9 254.2 %copy-start = (f32[1536]{0:T(1024)S(1)}, f32[1536]{0:T(1024)}, u32[]{:S(2)}) copy-start(f32[1536]{0:T(1024)} %param.7) | copy-start | bytes 18436
